TPU v7x, 32 devices: a whole 2x2x4 slice. The times are simulated.
32 devices in a mesh: groups: 2 (over y), ctx: 4 (over z), tensor: 2 (over x), dp: 2 (over core).
Axes of the slice: x: 2, y: 2, z: 4, core: 2. Of those that a mesh axis runs over, the one named last changes fastest.
Arguments:
- tokens: bfloat16 [4, 1024, 1024], P(('groups', 'dp'), 'ctx', 'tensor'), parts along dimension 0
- w_qkv: bfloat16 [1024, 3, 1024], P(None, None, 'tensor')
- w_out: bfloat16 [1024, 1024], P('tensor'), may hold values from -0.1875 to 0.1875
- labels: int32 [4, 8, 1024], P(('groups', 'dp'), 'tensor', 'ctx'), parts along dimension 0, may hold values from 0 to 255, as said below
- grad_out: bfloat16 [4, 1024, 1024], P(('groups', 'dp'), 'ctx', 'tensor'), parts along dimension 0, may hold values from -6 to 6
Outputs:
- attended: bfloat16 [4, 1024, 1024], P(('groups', 'dp'), 'ctx', 'tensor'), parts along dimension 0
- grad_tokens: bfloat16 [4, 1024, 1024], P(('groups', 'dp'), 'ctx', 'tensor'), parts along dimension 0
- grad_w_qkv: float32 [2048, 3, 1024], P('groups', None, 'tensor'), parts along dimension 0
- grad_w_out: float32 [2048, 1024], P(('groups', 'tensor')), parts along dimension 0
There are 2 independent parts, one for each index of `groups`. A program takes and returns all parts, laid end to end along the dimension named above; an argument that names none is the same for every part. Nothing has to cross between parts.
Inputs may be any that keep to these rules, and one draw needn't show every extreme that they name: `labels`: cluster c of any head belongs to owner c % 4. Among the 256 tokens of one document on one index of ctx, at most 192 have, for one head, clusters of one owner; for each head one owner has exactly 192 from every such block, and the other owners share the rest of a block evenly (counts differ by at most one).
All inputs are finite; a program needn't handle non-finite values.
Results may differ from a plain program's by a relative error of at most 0.035.
The roundings to bfloat16 on the way count: a program that leaves them out, or rounds other values in their place, can miss the bound.
Values may be sent and summed in bfloat16 or wider, within the bound.
A program may use at most 64 MiB of HBM per device.

v0:
```python
import math
import jax
import jax.numpy as jnp
from jax import lax
from jax.sharding import PartitionSpec as P

HD = 128


def contract_last(left, right):
    return lax.dot_general(
        left, right, (((1,), (1,)), ((), ())), preferred_element_type=jnp.float32
    )


def contract_first(left, right):
    return lax.dot_general(
        left, right, (((0,), (0,)), ((), ())), preferred_element_type=jnp.float32
    )


def masked_probs(query_block, label_block, keys_in, marks):
    scores = contract_last(query_block, keys_in) * HD ** (-0.5)
    same = label_block[:, None] == marks[None, :]
    scores = jnp.where(same, scores, jnp.float32(-1e30))
    top_value = jnp.max(scores, axis=1, keepdims=True)
    expo = jnp.exp(scores - top_value)
    return expo / jnp.sum(expo, axis=1, keepdims=True)


def owner_forward(queries, keys_in, values_in, marks):
    total = queries.shape[0]
    block_rows = math.gcd(total, 512)
    block_count = total // block_rows

    def forward_block(index):
        start = index * block_rows
        query_block = lax.dynamic_slice_in_dim(queries, start, block_rows, 0)
        label_block = lax.dynamic_slice_in_dim(marks, start, block_rows, 0)
        probs = masked_probs(query_block, label_block, keys_in, marks).astype(jnp.bfloat16)
        return jnp.dot(probs, values_in, preferred_element_type=jnp.float32).astype(jnp.bfloat16)

    return lax.map(forward_block, jnp.arange(block_count, dtype=jnp.int32)).reshape(
        total, queries.shape[1]
    )


def owner_backward(queries, keys_in, values_in, marks, attention, cotangent):
    total, size = queries.shape
    block_rows = math.gcd(total, 512)
    block_count = total // block_rows

    def backward_block(carry, index):
        grad_keys, grad_values = carry
        start = index * block_rows
        query_block = lax.dynamic_slice_in_dim(queries, start, block_rows, 0)
        label_block = lax.dynamic_slice_in_dim(marks, start, block_rows, 0)
        attn_block = lax.dynamic_slice_in_dim(attention, start, block_rows, 0)
        cot_block = lax.dynamic_slice_in_dim(cotangent, start, block_rows, 0)
        probs_full = masked_probs(query_block, label_block, keys_in, marks)
        probs = probs_full.astype(jnp.bfloat16)
        dprob = contract_last(cot_block, values_in)
        delta = jnp.sum(
            cot_block.astype(jnp.float32) * attn_block.astype(jnp.float32), axis=1, keepdims=True
        )
        dscore = (probs_full * (dprob - delta) * HD ** (-0.5)).astype(jnp.bfloat16)
        grad_query = jnp.dot(dscore, keys_in, preferred_element_type=jnp.float32).astype(
            jnp.bfloat16
        )
        grad_keys = grad_keys + contract_first(dscore, query_block)
        grad_values = grad_values + contract_first(probs, cot_block)
        return ((grad_keys, grad_values), grad_query)

    empty = jnp.zeros((total, size), jnp.float32)
    (grad_keys, grad_values), grad_queries = lax.scan(
        backward_block, (empty, empty), jnp.arange(block_count, dtype=jnp.int32)
    )
    return (
        grad_queries.reshape(total, size),
        grad_keys.astype(jnp.bfloat16),
        grad_values.astype(jnp.bfloat16),
    )


def shards(tokens, w_qkv, w_out, labels, grad_out):
    rows_all, grads_all = (
        lax.all_gather(tokens, "tensor", axis=2, tiled=True),
        lax.all_gather(grad_out, "tensor", axis=2, tiled=True),
    )
    tok_rows = rows_all[0]
    tok_grads = grads_all[0]
    tok_count, width = tok_rows.shape
    heads_local = w_out.shape[0] // HD
    ctx_count = lax.axis_size("ctx")
    capacity = 3 * tok_count // ctx_count
    slot_total = ctx_count * capacity
    qkv = jnp.dot(
        tok_rows, w_qkv.reshape(width, 3 * heads_local * HD), preferred_element_type=jnp.float32
    )
    qkv = qkv.astype(jnp.bfloat16).reshape(tok_count, 3, heads_local, HD)
    qkv_heads = jnp.transpose(qkv, (2, 0, 1, 3)).reshape(heads_local, tok_count, 3 * HD)
    cotangent = contract_last(tok_grads, w_out).astype(jnp.bfloat16)
    cot_heads = jnp.transpose(cotangent.reshape(tok_count, heads_local, HD), (1, 0, 2))
    labels_local = labels[0]
    owner_of = labels_local % ctx_count
    owner_hits = (
        owner_of[:, :, None] == jnp.arange(ctx_count, dtype=jnp.int32)[None, None, :]
    ).astype(jnp.int32)
    earlier = jnp.cumsum(owner_hits, axis=1) - owner_hits
    slot_index = jnp.sum(earlier * owner_hits, axis=2)
    destination = owner_of * capacity + slot_index

    def pack(values):
        feature_count = values.shape[2]
        empty_buffer = jnp.zeros((heads_local, slot_total, feature_count), values.dtype)
        filled = jax.vmap(lambda buffer, where_to, rows_in: buffer.at[where_to].set(rows_in))(
            empty_buffer, destination, values
        )
        return filled.reshape(heads_local, ctx_count, capacity, feature_count)

    def unpack(received):
        flat = received.reshape(heads_local, slot_total, received.shape[3])
        return jax.vmap(lambda table, where_to: jnp.take(table, where_to, axis=0))(
            flat, destination
        )

    label_slots = jax.vmap(
        lambda where_to, marks: jnp.full((slot_total,), -1.0, jnp.bfloat16).at[where_to].set(marks)
    )(destination, labels_local.astype(jnp.bfloat16)).reshape(heads_local, ctx_count, capacity)
    arrived, arrived_marks = (
        lax.all_to_all(pack(qkv_heads), "ctx", split_axis=1, concat_axis=1, tiled=True),
        lax.all_to_all(label_slots, "ctx", split_axis=1, concat_axis=1, tiled=True),
    )
    arrived = arrived.reshape(heads_local, slot_total, 3 * HD)
    marks_own = arrived_marks.reshape(heads_local, slot_total)
    queries_own = arrived[:, :, :HD]
    keys_own = arrived[:, :, HD : 2 * HD]
    values_own = arrived[:, :, 2 * HD :]
    attention_own = jax.vmap(owner_forward)(queries_own, keys_own, values_own, marks_own)
    returned = lax.all_to_all(
        attention_own.reshape(heads_local, ctx_count, capacity, HD),
        "ctx",
        split_axis=1,
        concat_axis=1,
        tiled=True,
    )
    attention_tok = unpack(returned)
    cot_arrived = lax.all_to_all(pack(cot_heads), "ctx", split_axis=1, concat_axis=1, tiled=True)
    cot_own = cot_arrived.reshape(heads_local, slot_total, HD)
    grad_q, grad_k, grad_v = jax.vmap(owner_backward)(
        queries_own, keys_own, values_own, marks_own, attention_own, cot_own
    )
    grads_own = jnp.concatenate([grad_q, grad_k, grad_v], axis=2).reshape(
        heads_local, ctx_count, capacity, 3 * HD
    )
    grads_back = lax.all_to_all(grads_own, "ctx", split_axis=1, concat_axis=1, tiled=True)
    grad_heads = unpack(grads_back)
    attention_rows = jnp.transpose(attention_tok, (1, 0, 2)).reshape(tok_count, heads_local * HD)
    out_terms = jnp.dot(attention_rows, w_out, preferred_element_type=jnp.float32)
    attended = lax.psum_scatter(
        out_terms.astype(jnp.bfloat16), "tensor", scatter_dimension=1, tiled=True
    )
    grad_qkv = jnp.transpose(grad_heads.reshape(heads_local, tok_count, 3, HD), (1, 2, 0, 3))
    grad_qkv = grad_qkv.reshape(tok_count, 3 * heads_local * HD)
    grad_w_out_local = contract_first(attention_rows, tok_grads)
    grad_w_qkv_local = contract_first(tok_rows, grad_qkv).reshape(width, 3, heads_local * HD)
    summed_qkv, summed_out = (
        lax.psum(grad_w_qkv_local.astype(jnp.bfloat16), ("ctx", "dp")).astype(jnp.float32),
        lax.psum(grad_w_out_local.astype(jnp.bfloat16), ("ctx", "dp")).astype(jnp.float32),
    )
    in_terms = contract_last(grad_qkv, w_qkv.reshape(width, 3 * heads_local * HD))
    grad_tokens = lax.psum_scatter(
        in_terms.astype(jnp.bfloat16), "tensor", scatter_dimension=1, tiled=True
    )
    return (attended[None], grad_tokens[None], summed_qkv, summed_out)


def solution(mesh):
    placed = (
        P(("groups", "dp"), "ctx", "tensor"),
        P(None, None, "tensor"),
        P("tensor", None),
        P(("groups", "dp"), "tensor", "ctx"),
        P(("groups", "dp"), "ctx", "tensor"),
    )
    return jax.shard_map(
        shards,
        mesh=mesh,
        in_specs=placed,
        out_specs=(
            P(("groups", "dp"), "ctx", "tensor"),
            P(("groups", "dp"), "ctx", "tensor"),
            P("groups", None, "tensor"),
            P(("groups", "tensor"), None),
        ),
        check_vma=False,
    )
```

profile of v0, /device:TPU:0, one launch (start us, length us, event | category | flops | bytes accessed | tf_op | source)
XLA Modules:
  0.0 419.2 jit_solution(18375576288930993019)
XLA Ops:
  10.2 4.8 %reduce-window.6 = s32[4,4,2,128]{3,2,1,0:T(2,128)S(1)} reduce-window(s32[4,4,2,128]{3,2,1,0:T(2,128)S(1)} %compare_convert_fusion, s32[]{:T(128)} %constant.96.clone.1), window={size=1x1x1x128 pad=0_0x0_0x0_0x127_0}, to_apply=%region_0.1 | reduce-window | flops 520192 | bytes 32772 | tf_op jit(solution)/shard_map/reduce-window
  17.8 7.6 %scatter_custom_fusion = bf16[3072]{0:T(1024)(128)(2,1)S(1)} fusion(s32[1024]{0:T(1024)S(1)} %bitcast.228, bf16[1024]{0:T(1024)(128)(2,1)S(1)} %bitcast.231, bf16[]{:T(256)} %constant.103.clone.1), kind=kCustom, calls=%fused_computation.120 | custom fusion | bytes 6146
  26.1 6.3 %all-to-all-start = ((bf16[4,4,192]{2,0,1:T(4,128)(2,1)}), bf16[4,4,192]{2,0,1:T(4,128)(2,1)S(1)}, u32[]{:S(2)}, u32[]{:S(2)}) async-start(bf16[4,4,192]{2,0,1:T(4,128)(2,1)} %copy.67), calls=%async_computation | async-start | bytes 16384 | tf_op jit(solution)/shard_map/all_to_all | solution.py:132
  32.4 8.6 %all_gather.7 = bf16[1,256,1024]{2,1,0:T(8,128)(2,1)S(1)} all-gather(bf16[1,256,512]{2,1,0:T(8,128)(2,1)} %param.13), channel_id=1, replica_groups=mesh['groups'=2,'ctx'=4,'tensor'=2,'dp'=2] {'tensor'}, dimensions={2}, use_global_device_ids=true | all-gather | bytes 786432 | tf_op jit(solution)/shard_map/all_gather | solution.py:88
  42.4 3.4 scatter_custom_fusion.2
  46.8 4.8 %all-to-all-start.3 = ((bf16[4,4,192,128]{3,2,0,1:T(8,128)(2,1)}), bf16[4,4,192,128]{3,2,0,1:T(8,128)(2,1)}, u32[]{:S(2)}, u32[]{:S(2)}) async-start(bf16[4,4,192,128]{3,2,0,1:T(8,128)(2,1)} %copy.80), calls=%async_computation.4 | async-start | bytes 1572864 | tf_op jit(solution)/shard_map/all_to_all | solution.py:148
  51.6 4.7 %copy.69 = bf16[1024,3,512]{0,2,1:T(8,128)(2,1)} copy(bf16[1024,3,512]{2,0,1:T(8,128)(2,1)} %param.10) | data formatting | bytes 6291456 | tf_op args[1]
  56.3 7.0 %all_gather.6 = bf16[1,256,1024]{2,1,0:T(8,128)(2,1)S(1)} all-gather(bf16[1,256,512]{2,1,0:T(8,128)(2,1)S(1)} %copy-done.10), channel_id=1, replica_groups=mesh['groups'=2,'ctx'=4,'tensor'=2,'dp'=2] {'tensor'}, dimensions={2}, use_global_device_ids=true | all-gather | bytes 786432 | tf_op jit(solution)/shard_map/all_gather | solution.py:87
  64.1 2.9 convolution_convert_fusion.2
  69.3 6.5 %scatter_custom_fusion.1 = bf16[3072,384]{1,0:T(8,128)(2,1)S(1)} fusion(s32[1024]{0:T(1024)S(1)} %bitcast.230, bf16[1024,384]{1,0:T(8,128)(2,1)} %copy.71, bf16[]{:T(256)} %constant.102.clone.1), kind=kCustom, calls=%fused_computation.77 | custom fusion | bytes 2359808
  75.8 1.7 copy.72
  77.5 5.1 %all-to-all-start.1 = ((bf16[4,4,192,384]{3,2,0,1:T(8,128)(2,1)}), bf16[4,4,192,384]{3,2,0,1:T(8,128)(2,1)}, u32[]{:S(2)}, u32[]{:S(2)}) async-start(bf16[4,4,192,384]{3,2,0,1:T(8,128)(2,1)} %copy.72), calls=%async_computation.1 | async-start | bytes 4718592 | tf_op jit(solution)/shard_map/all_to_all | solution.py:131
  82.9 2.1 copy.81
  85.0 48.7 %all-to-all-done.1 = bf16[4,4,192,384]{3,2,0,1:T(8,128)(2,1)} async-done(((bf16[4,4,192,384]{3,2,0,1:T(8,128)(2,1)}), bf16[4,4,192,384]{3,2,0,1:T(8,128)(2,1)}, u32[]{:S(2)}, u32[]{:S(2)}) %all-to-all-start.1) | async-done | bytes 2359328 | tf_op jit(solution)/shard_map/all_to_all | solution.py:131
  133.7 1.9 copy.73
  137.4 23.0 %while.33 = (s32[]{:T(128)}, bf16[3,4,256,128]{3,2,0,1:T(8,128)(2,1)S(1)}, s32[3]{0:T(128)S(1)}, bf16[4,768]{1,0:T(4,128)(2,1)S(1)}, bf16[4,4,192]{2,1,0:T(4,128...) while((s32[]{:T(128)}, ...), condition=%wide.wide.region_8.9_spmd, body=%wide.wide.region_5.8_spmd.sunk | while | flops 612764160 | bytes 3175139 | solution.py:43
  138.8 2.5 fusion.172
  141.3 3.8 fusion.173
  146.5 2.5 fusion.172
  149.0 3.8 fusion.173
  154.1 2.5 fusion.172
  156.6 3.8 fusion.173
  161.4 4.2 all-to-all-start.2
  166.7 56.3 %while.34 = (s32[]{:T(128)}, f32[4,768,128]{2,1,0:T(8,128)S(1)}, f32[4,768,128]{2,1,0:T(8,128)}, bf16[3,4,256,128]{3,2,0,1:T(8,128)(2,1)}, s32[3]{0:T(128)S(1)},...) while((s32[]{:T(128)}, f32[4,768,128]{2,1,0:T(8,128)S(1)}, ...), condition=%wide.wide.region_15.16_spmd.clone, body=%wide.wide.region_11.15_spmd.clone.sunk | while | flops 1222772224 | bytes 25732404 | solution.py:75
  169.2 4.1 fusion.187
  173.3 3.0 multiply_convert_fusion.3
  177.6 2.2 select_add_fusion.6
  179.9 5.2 %select_add_fusion.7 = f32[4,768,128]{2,1,0:T(8,128)} fusion(f32[4,768,128]{2,1,0:T(8,128)} %get-tuple-element.590, f32[4,256]{1,0:T(4,128)S(1)} %get-tuple-element.527, pred[]{:T(512)S(6)} %compare.29, bf16[4,768,128]{2,1,0:T(8,128)(2,1)} %get-tuple-element.615, s32[]{:T(128)S(1)} %bitcast.226, ...), kind=kOutput, calls=%fused_computation.37.clone.clone.1 | convolution fusion | flops 408160000 | bytes 4469761 | tf_op jit(solution)/shard_map/vmap()/while/body/eval_jaxpr/dot_general | solution.py:17
  187.6 4.1 fusion.187
  191.7 3.0 multiply_convert_fusion.3
  196.0 2.2 select_add_fusion.6
  198.3 5.7 %select_add_fusion.7 = f32[4,768,128]{2,1,0:T(8,128)} fusion(f32[4,768,128]{2,1,0:T(8,128)} %get-tuple-element.590, f32[4,256]{1,0:T(4,128)S(1)} %get-tuple-element.527, pred[]{:T(512)S(6)} %compare.29, bf16[4,768,128]{2,1,0:T(8,128)(2,1)} %get-tuple-element.615, s32[]{:T(128)S(1)} %bitcast.226, ...), kind=kOutput, calls=%fused_computation.37.clone.clone.1 | convolution fusion | flops 408160000 | bytes 4469761 | tf_op jit(solution)/shard_map/vmap()/while/body/eval_jaxpr/dot_general | solution.py:17
  206.6 4.1 fusion.187
  210.7 3.0 multiply_convert_fusion.3
  215.0 2.2 select_add_fusion.6
  217.2 5.7 %select_add_fusion.7 = f32[4,768,128]{2,1,0:T(8,128)} fusion(f32[4,768,128]{2,1,0:T(8,128)} %get-tuple-element.590, f32[4,256]{1,0:T(4,128)S(1)} %get-tuple-element.527, pred[]{:T(512)S(6)} %compare.29, bf16[4,768,128]{2,1,0:T(8,128)(2,1)} %get-tuple-element.615, s32[]{:T(128)S(1)} %bitcast.226, ...), kind=kOutput, calls=%fused_computation.37.clone.clone.1 | convolution fusion | flops 408160000 | bytes 4469761 | tf_op jit(solution)/shard_map/vmap()/while/body/eval_jaxpr/dot_general | solution.py:17
  226.0 1.7 copy.84
  227.6 5.2 %all-to-all-start.4 = ((bf16[4,4,192,384]{3,2,0,1:T(8,128)(2,1)}), bf16[4,4,192,384]{3,2,0,1:T(8,128)(2,1)}, u32[]{:S(2)}, u32[]{:S(2)}) async-start(bf16[4,4,192,384]{3,2,0,1:T(8,128)(2,1)} %copy.84), calls=%async_computation.5 | async-start | bytes 4718592 | tf_op jit(solution)/shard_map/all_to_all | solution.py:156
  234.1 5.8 %gather_fusion = bf16[1024,128]{1,0:T(8,128)(2,1)S(1)} fusion(bf16[4,768,128]{2,1,0:T(8,128)(2,1)S(1)} %bitcast.205, s32[1024]{0:T(1024)S(1)} %bitcast.199), kind=kCustom, calls=%fused_computation | custom fusion | bytes 532480 | tf_op jit(solution)/shard_map/vmap(jit(_take))/gather | solution.py:123
  242.3 43.4 %all-to-all-done.4 = bf16[4,4,192,384]{3,2,0,1:T(8,128)(2,1)} async-done(((bf16[4,4,192,384]{3,2,0,1:T(8,128)(2,1)}), bf16[4,4,192,384]{3,2,0,1:T(8,128)(2,1)}, u32[]{:S(2)}, u32[]{:S(2)}) %all-to-all-start.4) | async-done | bytes 2359328 | tf_op jit(solution)/shard_map/all_to_all | solution.py:156
  285.7 1.9 copy.85
  287.6 11.6 %gather_fusion.1 = bf16[1024,384]{1,0:T(8,128)(2,1)} fusion(bf16[4,768,384]{2,1,0:T(8,128)(2,1)S(1)} %bitcast.201, s32[1024]{0:T(1024)S(1)} %bitcast.200), kind=kCustom, calls=%fused_computation.1 | custom fusion | bytes 1581056 | tf_op jit(solution)/shard_map/vmap(jit(_take))/gather | solution.py:123
  301.7 2.7 convolution_convert_fusion.1
  304.4 4.7 %copy.88 = bf16[1024,3,512]{2,0,1:T(8,128)(2,1)} copy(bf16[1024,3,512]{0,2,1:T(8,128)(2,1)} %bitcast.202) | data formatting | bytes 6291456 | tf_op jit(solution)/shard_map/convert_element_type | solution.py:168
  311.3 3.7 convolution_convert_fusion.5
  315.1 90.2 %all-reduce.3.cloned.1.call-done = (bf16[1024,3,512]{2,0,1:T(8,128)(2,1)}, bf16[512,1024]{1,0:T(8,128)(2,1)}) async-done(((bf16[1024,3,512]{2,0,1:T(8,128)(2,1)}, bf16[512,1024]{1,0:T(8,128)(2,1)}), (bf16[1024,3,512]{2,0,1:T(8,128)(2,1)}, bf16[512,1024]{1,0:T(8,128)(2,1)})) %all-reduce.3.cloned.1.call-update) | async-done | bytes 4194320 | tf_op jit(solution)/shard_map/psum | solution.py:168
  405.3 2.9 convert_element_type.81
  408.2 3.6 convert_element_type.79
  (120 shorter events, 37.9 us)
Async XLA Ops:
  8.0 33.8 %copy-start = (bf16[512,1024]{1,0:T(8,128)(2,1)S(1)}, bf16[512,1024]{1,0:T(8,128)(2,1)}, u32[]{:S(2)}) copy-start(bf16[512,1024]{1,0:T(8,128)(2,1)} %param.11) | copy-start | bytes 3145732
  26.1 20.7 %all-to-all-start = ((bf16[4,4,192]{2,0,1:T(4,128)(2,1)}), bf16[4,4,192]{2,0,1:T(4,128)(2,1)S(1)}, u32[]{:S(2)}, u32[]{:S(2)}) async-start(bf16[4,4,192]{2,0,1:T(4,128)(2,1)} %copy.67), calls=%async_computation | async-start | bytes 16384 | tf_op jit(solution)/shard_map/all_to_all | solution.py:132
  41.0 0.8 copy-start.1
  46.8 30.7 %all-to-all-start.3 = ((bf16[4,4,192,128]{3,2,0,1:T(8,128)(2,1)}), bf16[4,4,192,128]{3,2,0,1:T(8,128)(2,1)}, u32[]{:S(2)}, u32[]{:S(2)}) async-start(bf16[4,4,192,128]{3,2,0,1:T(8,128)(2,1)} %copy.80), calls=%async_computation.4 | async-start | bytes 1572864 | tf_op jit(solution)/shard_map/all_to_all | solution.py:148
  51.6 4.7 %copy-start.10 = (bf16[1,256,512]{2,1,0:T(8,128)(2,1)S(1)}, bf16[1,256,512]{2,1,0:T(8,128)(2,1)}, u32[]{:S(2)}) copy-start(bf16[1,256,512]{2,1,0:T(8,128)(2,1)} %param.9) | copy-start | bytes 786436
  63.3 0.8 copy-start.6
  77.5 56.2 %all-to-all-start.1 = ((bf16[4,4,192,384]{3,2,0,1:T(8,128)(2,1)}), bf16[4,4,192,384]{3,2,0,1:T(8,128)(2,1)}, u32[]{:S(2)}, u32[]{:S(2)}) async-start(bf16[4,4,192,384]{3,2,0,1:T(8,128)(2,1)} %copy.72), calls=%async_computation.1 | async-start | bytes 4718592 | tf_op jit(solution)/shard_map/all_to_all | solution.py:131
  82.6 53.0 %copy-start.11 = (bf16[4,4,192]{2,1,0:T(4,128)(2,1)}, bf16[4,4,192]{2,1,0:T(4,128)(2,1)S(1)}, u32[]{:S(2)}) copy-start(bf16[4,4,192]{2,1,0:T(4,128)(2,1)S(1)} %copy.68) | copy-start | bytes 18436
  161.4 66.2 %all-to-all-start.2 = ((bf16[4,4,192,128]{3,2,0,1:T(8,128)(2,1)}), bf16[4,4,192,128]{3,2,0,1:T(8,128)(2,1)}, u32[]{:S(2)}, u32[]{:S(2)}) async-start(bf16[4,4,192,128]{3,2,0,1:T(8,128)(2,1)} %copy.76), calls=%async_computation.2 | async-start | bytes 1572864 | tf_op jit(solution)/shard_map/all_to_all | solution.py:140
  173.3 3.0 copy-start.9
  191.7 3.0 copy-start.9
  210.7 3.0 copy-start.9
  223.0 1.4 copy-start.8
  227.6 5.2 %copy-start.12 = (s32[1,4,256]{2,1,0:T(4,128)S(1)}, s32[1,4,256]{2,1,0:T(4,128)}, u32[]{:S(2)}) copy-start(s32[1,4,256]{2,1,0:T(4,128)} %param.12) | copy-start | bytes 12292
  227.6 58.0 %all-to-all-start.4 = ((bf16[4,4,192,384]{3,2,0,1:T(8,128)(2,1)}), bf16[4,4,192,384]{3,2,0,1:T(8,128)(2,1)}, u32[]{:S(2)}, u32[]{:S(2)}) async-start(bf16[4,4,192,384]{3,2,0,1:T(8,128)(2,1)} %copy.84), calls=%async_computation.5 | async-start | bytes 4718592 | tf_op jit(solution)/shard_map/all_to_all | solution.py:156
  232.8 8.0 %copy-start.2 = (bf16[1,256,1024]{2,1,0:T(8,128)(2,1)S(1)}, bf16[1,256,1024]{2,1,0:T(8,128)(2,1)}, u32[]{:S(2)}) copy-start(bf16[1,256,1024]{2,1,0:T(8,128)(2,1)} %copy-done.1) | copy-start | bytes 1572868
  232.8 172.4 %all-reduce.3.cloned.1.call-start = ((), (), s32[]{:S(2)}) async-start(), calls=%async_computation.9 | async-start | bytes 8388608 | tf_op jit(solution)/shard_map/psum | solution.py:168
  240.2 0.7 copy-start.4
  299.2 2.5 copy-start.7
  309.1 0.9 copy-start.5
  309.1 102.7 %reduce-scatter.3.cloned.1.call-start = ((), (), s32[]{:S(2)}) async-start(), calls=%async_computation.7 | async-start | bytes 786432 | tf_op jit(solution)/shard_map/reduce_scatter | solution.py:160
  311.3 100.5 %reduce-scatter.5.cloned.1.call-start = ((), (), s32[]{:S(2)}) async-start(), calls=%async_computation.8 | async-start | bytes 786432 | tf_op jit(solution)/shard_map/reduce_scatter | solution.py:172
  405.2 2.9 copy-start.3
Sparse Core Ops, SparseCore 0:
  309.2 95.9 all-reduce.2
Sparse Core Ops, SparseCore 1:
  312.4 13.6 reduce-scatter.2
  328.8 14.5 reduce-scatter.4
where the time goes:
time: 421 us; the launch traced here: 419 us
  waiting for transfers between devices  182 us (43%)
  matrix products  80 us (19%)
  local copies, waits for them, and re-layouts  74.3 us (18%)
  starting transfers between devices  25.7 us (6%)
  other arithmetic  21.4 us (5%)
  between operations  15.8 us (4%)
  blocking collectives  15.7 us (4%)
    psum x1, waiting for transfers between devices, shards(): lax.psum(grad_w_qkv_local.astype(jnp.bfloat16), ('ctx', 'dp'))  90.2 us
    all_to_all x1, waiting for transfers between devices, shards(): lax.all_to_all(pack(qkv_heads), 'ctx', split_axis=1, concat_axis=1, tiled...  48.7 us
    all_to_all x1, waiting for transfers between devices, shards(): lax.all_to_all(grads_own, 'ctx', split_axis=1, concat_axis=1, tiled=True)  43.4 us
    dot_general x8, matrix products, contract_first(): lax.dot_general(left, right, (((0,), (0,)), ((), ())), preferred_element_...  27.5 us
    unnamed x32, local copies, waits for them, and re-layouts  26.9 us
    sub x6, matrix products, masked_probs(): expo = jnp.exp(scores - top_value)  19.8 us
    gather x5, local copies, waits for them, and re-layouts, unpack(): jnp.take(table, where_to, axis=0)  19.6 us
    dot_general x5, matrix products, contract_last(): lax.dot_general(left, right, (((1,), (1,)), ((), ())), preferred_element_...  13.2 us
  transfers between devices with their start and end apart: 8, of which 3 were waited for; matrix products, arithmetic and copies ran while one was open for 25% of the time, Pallas kernels for 0%

commit v1 on v0

--- a/solution.py
+++ b/solution.py
@@ -165,7 +165,7 @@
     grad_w_out_local = contract_first(attention_rows, tok_grads)
     grad_w_qkv_local = contract_first(tok_rows, grad_qkv).reshape(width, 3, heads_local * HD)
     summed_qkv, summed_out = (
-        lax.psum(grad_w_qkv_local.astype(jnp.bfloat16), ("ctx", "dp")).astype(jnp.float32),
+        lax.psum(lax.psum(grad_w_qkv_local.astype(jnp.bfloat16), "dp"), "ctx").astype(jnp.float32),
         lax.psum(grad_w_out_local.astype(jnp.bfloat16), ("ctx", "dp")).astype(jnp.float32),
     )
     in_terms = contract_last(grad_qkv, w_qkv.reshape(width, 3 * heads_local * HD))

time: 421 us -> 530 us (1.26)
  waiting for transfers between devices: 182 us -> 275 us
  blocking collectives: 15.7 us -> 37.7 us
    psum x1 -> x3, waiting for transfers between devices: 90.2 us -> 172 us  [the longest x1 120 us: shards(): lax.psum(lax.psum(grad_w_qkv_local.astype(jnp.bfloat16), 'dp'), 'ctx')]
    all_to_all x0 -> x1, blocking collectives: none -> 22.1 us  [shards(): lax.all_to_all(attention_own.reshape(heads_local, ctx_count, capacity, HD...]
    all_to_all x1, waiting for transfers between devices: 43.4 us -> 53.1 us  [shards(): lax.all_to_all(grads_own, 'ctx', split_axis=1, concat_axis=1, tiled=True)]
    unnamed x32 -> x30, local copies, waits for them, and re-layouts: 26.9 us -> 26.7 us
  transfers between devices with their start and end apart: 8 -> 9, of which waited for: 3 -> 4; matrix products, arithmetic and copies ran while one was open for 25% -> 9% of each run, Pallas kernels for 0% -> 0%
where the time goes in v1:
time: 530 us; the launch traced here: 528 us
  waiting for transfers between devices  275 us (52%)
  matrix products  79.9 us (15%)
  local copies, waits for them, and re-layouts  72.2 us (14%)
  blocking collectives  37.7 us (7%)
  other arithmetic  23.1 us (4%)
  starting transfers between devices  21.3 us (4%)
  between operations  15.5 us (3%)
    psum x1, waiting for transfers between devices, shards(): lax.psum(lax.psum(grad_w_qkv_local.astype(jnp.bfloat16), 'dp'), 'ctx')  120 us
    all_to_all x1, waiting for transfers between devices, shards(): lax.all_to_all(grads_own, 'ctx', split_axis=1, concat_axis=1, tiled=True)  53.1 us
    psum x1, waiting for transfers between devices, shards(): lax.psum(grad_w_out_local.astype(jnp.bfloat16), ('ctx', 'dp'))  52.2 us
    all_to_all x1, waiting for transfers between devices, shards(): lax.all_to_all(pack(qkv_heads), 'ctx', split_axis=1, concat_axis=1, tiled...  48.8 us
    dot_general x8, matrix products, contract_first(): lax.dot_general(left, right, (((0,), (0,)), ((), ())), preferred_element_...  27.4 us
    unnamed x30, local copies, waits for them, and re-layouts  26.7 us
    all_to_all x1, blocking collectives, shards(): lax.all_to_all(attention_own.reshape(heads_local, ctx_count, capacity, HD...  22.1 us
    sub x6, matrix products, masked_probs(): expo = jnp.exp(scores - top_value)  19.8 us
  transfers between devices with their start and end apart: 9, of which 4 were waited for; matrix products, arithmetic and copies ran while one was open for 9% of the time, Pallas kernels for 0%

profile of v1, /device:TPU:0, one launch (start us, length us, event | category | flops | bytes accessed | tf_op | source)
XLA Modules:
  0.0 528.3 jit_solution(6833130238845513944)
XLA Ops:
  10.2 4.8 reduce-window.6
  17.8 7.6 %scatter_custom_fusion = bf16[3072]{0:T(1024)(128)(2,1)S(1)} fusion(s32[1024]{0:T(1024)S(1)} %bitcast.228, bf16[1024]{0:T(1024)(128)(2,1)S(1)} %bitcast.231, bf16[]{:T(256)} %constant.103.clone.1), kind=kCustom, calls=%fused_computation.120 | custom fusion | bytes 6146
  26.1 6.3 %all-to-all-start = ((bf16[4,4,192]{2,0,1:T(4,128)(2,1)}), bf16[4,4,192]{2,0,1:T(4,128)(2,1)S(1)}, u32[]{:S(2)}, u32[]{:S(2)}) async-start(bf16[4,4,192]{2,0,1:T(4,128)(2,1)} %copy.67), calls=%async_computation | async-start | bytes 16384 | tf_op jit(solution)/shard_map/all_to_all | solution.py:132
  32.4 8.6 %all_gather.7 = bf16[1,256,1024]{2,1,0:T(8,128)(2,1)S(1)} all-gather(bf16[1,256,512]{2,1,0:T(8,128)(2,1)} %param.13), channel_id=1, replica_groups=mesh['groups'=2,'ctx'=4,'tensor'=2,'dp'=2] {'tensor'}, dimensions={2}, use_global_device_ids=true | all-gather | bytes 786432 | tf_op jit(solution)/shard_map/all_gather | solution.py:88
  42.4 3.4 scatter_custom_fusion.2
  46.8 4.8 all-to-all-start.3
  51.6 4.7 copy.69
  56.3 7.0 %all_gather.6 = bf16[1,256,1024]{2,1,0:T(8,128)(2,1)S(1)} all-gather(bf16[1,256,512]{2,1,0:T(8,128)(2,1)S(1)} %copy-done.9), channel_id=1, replica_groups=mesh['groups'=2,'ctx'=4,'tensor'=2,'dp'=2] {'tensor'}, dimensions={2}, use_global_device_ids=true | all-gather | bytes 786432 | tf_op jit(solution)/shard_map/all_gather | solution.py:87
  64.1 2.9 convolution_convert_fusion.2
  69.3 6.5 %scatter_custom_fusion.1 = bf16[3072,384]{1,0:T(8,128)(2,1)S(1)} fusion(s32[1024]{0:T(1024)S(1)} %bitcast.230, bf16[1024,384]{1,0:T(8,128)(2,1)} %copy.71, bf16[]{:T(256)} %constant.102.clone.1), kind=kCustom, calls=%fused_computation.77 | custom fusion | bytes 2359808
  75.8 1.7 copy.72
  77.5 5.1 all-to-all-start.1
  82.9 2.1 copy.81
  85.0 48.8 %all-to-all-done.1 = bf16[4,4,192,384]{3,2,0,1:T(8,128)(2,1)} async-done(((bf16[4,4,192,384]{3,2,0,1:T(8,128)(2,1)}), bf16[4,4,192,384]{3,2,0,1:T(8,128)(2,1)}, u32[]{:S(2)}, u32[]{:S(2)}) %all-to-all-start.1) | async-done | bytes 2359328 | tf_op jit(solution)/shard_map/all_to_all | solution.py:131
  133.7 1.9 copy.73
  137.4 23.1 %while.33 = (s32[]{:T(128)}, bf16[3,4,256,128]{3,2,0,1:T(8,128)(2,1)S(1)}, s32[3]{0:T(128)S(1)}, bf16[4,768]{1,0:T(4,128)(2,1)S(1)}, bf16[4,4,192]{2,1,0:T(4,128...) while((s32[]{:T(128)}, ...), condition=%wide.wide.region_8.9_spmd, body=%wide.wide.region_5.8_spmd.sunk | while | flops 612764160 | bytes 3175139 | solution.py:43
  138.8 2.5 fusion.172
  141.3 3.8 fusion.173
  146.5 2.5 fusion.172
  149.0 3.8 fusion.173
  154.3 2.5 fusion.172
  156.8 3.8 fusion.173
  161.6 56.3 %while.34 = (s32[]{:T(128)}, f32[4,768,128]{2,1,0:T(8,128)S(1)}, f32[4,768,128]{2,1,0:T(8,128)}, bf16[3,4,256,128]{3,2,0,1:T(8,128)(2,1)}, s32[3]{0:T(128)S(1)},...) while((s32[]{:T(128)}, f32[4,768,128]{2,1,0:T(8,128)S(1)}, ...), condition=%wide.wide.region_15.16_spmd.clone, body=%wide.wide.region_11.15_spmd.clone.sunk | while | flops 1222772224 | bytes 25732404 | solution.py:75
  164.2 4.1 fusion.187
  168.3 3.0 multiply_convert_fusion.3
  172.6 2.2 select_add_fusion.6
  174.8 5.2 select_add_fusion.7
  182.6 4.1 fusion.187
  186.7 3.0 multiply_convert_fusion.3
  191.0 2.2 select_add_fusion.6
  193.2 5.7 %select_add_fusion.7 = f32[4,768,128]{2,1,0:T(8,128)} fusion(f32[4,768,128]{2,1,0:T(8,128)} %get-tuple-element.588, f32[4,256]{1,0:T(4,128)S(1)} %get-tuple-element.525, pred[]{:T(512)S(6)} %compare.29, bf16[4,768,128]{2,1,0:T(8,128)(2,1)} %get-tuple-element.613, s32[]{:T(128)S(1)} %bitcast.226, ...), kind=kOutput, calls=%fused_computation.37.clone.clone.1 | convolution fusion | flops 408160000 | bytes 4469761 | tf_op jit(solution)/shard_map/vmap()/while/body/eval_jaxpr/dot_general | solution.py:17
  201.5 4.1 fusion.187
  205.6 3.0 multiply_convert_fusion.3
  209.9 2.2 select_add_fusion.6
  212.2 5.7 %select_add_fusion.7 = f32[4,768,128]{2,1,0:T(8,128)} fusion(f32[4,768,128]{2,1,0:T(8,128)} %get-tuple-element.588, f32[4,256]{1,0:T(4,128)S(1)} %get-tuple-element.525, pred[]{:T(512)S(6)} %compare.29, bf16[4,768,128]{2,1,0:T(8,128)(2,1)} %get-tuple-element.613, s32[]{:T(128)S(1)} %bitcast.226, ...), kind=kOutput, calls=%fused_computation.37.clone.clone.1 | convolution fusion | flops 408160000 | bytes 4469761 | tf_op jit(solution)/shard_map/vmap()/while/body/eval_jaxpr/dot_general | solution.py:17
  222.8 4.6 all-to-all-start.4
  227.8 53.1 %all-to-all-done.4 = bf16[4,4,192,384]{3,2,0,1:T(8,128)(2,1)} async-done(((bf16[4,4,192,384]{3,2,0,1:T(8,128)(2,1)}), bf16[4,4,192,384]{3,2,0,1:T(8,128)(2,1)}, u32[]{:S(2)}, u32[]{:S(2)}) %all-to-all-start.4) | async-done | bytes 2359328 | tf_op jit(solution)/shard_map/all_to_all | solution.py:156
  280.8 1.9 copy.85
  282.7 11.6 %gather_fusion.1 = bf16[1024,384]{1,0:T(8,128)(2,1)} fusion(bf16[4,768,384]{2,1,0:T(8,128)(2,1)S(1)} %bitcast.201, s32[1024]{0:T(1024)S(1)} %bitcast.199), kind=kCustom, calls=%fused_computation.1 | custom fusion | bytes 1581056 | tf_op jit(solution)/shard_map/vmap(jit(_take))/gather | solution.py:123
  296.9 2.7 convolution_convert_fusion.1
  299.6 4.7 copy.88
  305.5 22.1 %all_to_all.25 = bf16[4,4,192,128]{3,2,0,1:T(8,128)(2,1)S(1)} all-to-all(bf16[4,4,192,128]{3,2,0,1:T(8,128)(2,1)S(1)} %copy.76), channel_id=1, replica_groups=mesh['groups'=2,'ctx'=4,'tensor'=2,'dp'=2] {'ctx'}, dimensions={1} | all-to-all | bytes 1572864 | tf_op jit(solution)/shard_map/all_to_all | solution.py:140
  327.6 5.8 %gather_fusion = bf16[1024,128]{1,0:T(8,128)(2,1)S(1)} fusion(bf16[4,768,128]{2,1,0:T(8,128)(2,1)S(1)} %bitcast.205, s32[1024]{0:T(1024)S(1)} %bitcast.200), kind=kCustom, calls=%fused_computation | custom fusion | bytes 532480 | tf_op jit(solution)/shard_map/vmap(jit(_take))/gather | solution.py:123
  337.2 3.7 convolution_convert_fusion.5
  340.9 52.2 %all-reduce.8.cloned.1.call-done = bf16[512,1024]{1,0:T(8,128)(2,1)} async-done(((bf16[512,1024]{1,0:T(8,128)(2,1)}), bf16[512,1024]{1,0:T(8,128)(2,1)}) %all-reduce.8.cloned.1.call-update) | async-done | bytes 1048592 | tf_op jit(solution)/shard_map/psum | solution.py:169
  393.1 2.8 convert_element_type.81
  395.9 119.8 %all-reduce.6.cloned.1.call-done = bf16[1024,3,512]{2,0,1:T(8,128)(2,1)} async-done(((bf16[1024,3,512]{2,0,1:T(8,128)(2,1)}), bf16[1024,3,512]{2,0,1:T(8,128)(2,1)}) %all-reduce.6.cloned.1.call-update) | async-done | bytes 3145744 | tf_op jit(solution)/shard_map/psum | solution.py:168
  515.7 5.5 %convert_element_type.79 = f32[1024,3,512]{2,0,1:T(8,128)} convert(bf16[1024,3,512]{2,0,1:T(8,128)(2,1)} %all-reduce.6.cloned.1.call-done) | non-fusion elementwise | flops 1572864 | bytes 9437184 | tf_op jit(solution)/shard_map/convert_element_type | solution.py:168
  (123 shorter events, 38.4 us)
Async XLA Ops:
  8.0 33.8 %copy-start = (bf16[512,1024]{1,0:T(8,128)(2,1)S(1)}, bf16[512,1024]{1,0:T(8,128)(2,1)}, u32[]{:S(2)}) copy-start(bf16[512,1024]{1,0:T(8,128)(2,1)} %param.11) | copy-start | bytes 3145732
  26.1 20.7 %all-to-all-start = ((bf16[4,4,192]{2,0,1:T(4,128)(2,1)}), bf16[4,4,192]{2,0,1:T(4,128)(2,1)S(1)}, u32[]{:S(2)}, u32[]{:S(2)}) async-start(bf16[4,4,192]{2,0,1:T(4,128)(2,1)} %copy.67), calls=%async_computation | async-start | bytes 16384 | tf_op jit(solution)/shard_map/all_to_all | solution.py:132
  41.0 0.8 copy-start.3
  46.8 30.7 %all-to-all-start.3 = ((bf16[4,4,192,128]{3,2,0,1:T(8,128)(2,1)}), bf16[4,4,192,128]{3,2,0,1:T(8,128)(2,1)}, u32[]{:S(2)}, u32[]{:S(2)}) async-start(bf16[4,4,192,128]{3,2,0,1:T(8,128)(2,1)} %copy.80), calls=%async_computation.4 | async-start | bytes 1572864 | tf_op jit(solution)/shard_map/all_to_all | solution.py:148
  51.6 4.7 copy-start.9
  63.3 0.8 copy-start.5
  77.5 56.2 %all-to-all-start.1 = ((bf16[4,4,192,384]{3,2,0,1:T(8,128)(2,1)}), bf16[4,4,192,384]{3,2,0,1:T(8,128)(2,1)}, u32[]{:S(2)}, u32[]{:S(2)}) async-start(bf16[4,4,192,384]{3,2,0,1:T(8,128)(2,1)} %copy.72), calls=%async_computation.1 | async-start | bytes 4718592 | tf_op jit(solution)/shard_map/all_to_all | solution.py:131
  82.6 53.0 %copy-start.10 = (bf16[4,4,192]{2,1,0:T(4,128)(2,1)}, bf16[4,4,192]{2,1,0:T(4,128)(2,1)S(1)}, u32[]{:S(2)}) copy-start(bf16[4,4,192]{2,1,0:T(4,128)(2,1)S(1)} %copy.68) | copy-start | bytes 18436
  168.3 3.0 copy-start.8
  186.7 3.0 copy-start.8
  205.6 3.0 copy-start.8
  217.9 3.3 copy-start.1
  217.9 1.7 copy-start.7
  222.8 4.9 copy-start.11
  222.8 58.0 %all-to-all-start.4 = ((bf16[4,4,192,384]{3,2,0,1:T(8,128)(2,1)}), bf16[4,4,192,384]{3,2,0,1:T(8,128)(2,1)}, u32[]{:S(2)}, u32[]{:S(2)}) async-start(bf16[4,4,192,384]{3,2,0,1:T(8,128)(2,1)} %copy.84), calls=%async_computation.5 | async-start | bytes 4718592 | tf_op jit(solution)/shard_map/all_to_all | solution.py:156
  227.5 107.7 %all-reduce.4.cloned.1.call-start = ((), (), s32[]{:S(2)}) async-start(), calls=%async_computation.9 | async-start | bytes 6291456 | tf_op jit(solution)/shard_map/psum | solution.py:168
  294.4 2.5 copy-start.6
  304.3 1.1 copy-start.2
  304.3 88.8 %all-reduce.8.cloned.1.call-start = ((), (), s32[]{:S(2)}) async-start(), calls=%async_computation.11 | async-start | bytes 2097152 | tf_op jit(solution)/shard_map/psum | solution.py:169
  327.5 6.1 %copy-start.4 = (bf16[1,256,1024]{2,1,0:T(8,128)(2,1)S(1)}, bf16[1,256,1024]{2,1,0:T(8,128)(2,1)}, u32[]{:S(2)}) copy-start(bf16[1,256,1024]{2,1,0:T(8,128)(2,1)} %copy-done.3) | copy-start | bytes 1572868
  335.1 180.6 %all-reduce.6.cloned.1.call-start = ((), (), s32[]{:S(2)}) async-start(), calls=%async_computation.10 | async-start | bytes 6291456 | tf_op jit(solution)/shard_map/psum | solution.py:168
  335.8 185.4 %reduce-scatter.3.cloned.1.call-start = ((), (), s32[]{:S(2)}) async-start(), calls=%async_computation.7 | async-start | bytes 786432 | tf_op jit(solution)/shard_map/reduce_scatter | solution.py:160
  337.1 184.1 %reduce-scatter.5.cloned.1.call-start = ((), (), s32[]{:S(2)}) async-start(), calls=%async_computation.8 | async-start | bytes 786432 | tf_op jit(solution)/shard_map/reduce_scatter | solution.py:172
Sparse Core Ops, SparseCore 0:
  304.4 22.3 all-reduce.3
  335.2 57.9 all-reduce.7
  395.6 120.0 all-reduce.5
Sparse Core Ops, SparseCore 1:
  339.1 13.5 reduce-scatter.2
  355.4 14.5 reduce-scatter.4
